TPU v7x, 128 devices: a whole 4x4x4 slice. The times are simulated.
128 devices in a mesh: shot: 16 (over y, x_lo, core), brick: 8 (over z, x_hi).
Axes of the slice: x: 4 (x_hi: 2, x_lo: 2; x = x_hi * 2 + x_lo), y: 4, z: 4, core: 2. Of those that a mesh axis runs over, the one named last changes fastest.
Arguments:
- latent: bfloat16 [16, 256, 32, 128], P(None, 'brick', 'shot'), may hold values from -6 to 6
- conv_in: bfloat16 [27, 16, 16], replicated, may hold values from -0.3125 to 0.3125
- conv_out: bfloat16 [27, 2, 16], replicated, may hold values from -0.3125 to 0.3125
- source_field: float32 [16, 256, 16, 128], P('shot', 'brick'), may hold values from -6 to 6
- observed: float32 [16, 3, 2048], P('shot'), may hold values from -6 to 6
- aperture: int32 [16], P('shot'), may hold values from 0 to 16, as said below
- receivers: int32 [16, 3, 2048], P('shot'), may hold values from 0 to 255, as said below
Outputs:
- grad_latent: float32 [16, 256, 32, 128], P(None, 'brick', 'shot')
- grad_first: float32 [27, 16, 16], replicated
- grad_second: float32 [27, 2, 16], replicated
Inputs may be any that keep to these rules, and one draw needn't show every extreme that they name: Every shot's aperture lies inside the grid; some shot starts at 0 and some at 16. `receivers`: each receiver's first index is below 256, its third below 128, and its second lies inside its shot's aperture.
All inputs are finite; a program needn't handle non-finite values.
Results may differ from a plain program's by a relative error of at most 0.0023.
The roundings to bfloat16 on the way count: a program that leaves them out, or rounds other values in their place, can miss the bound.
Values may be sent and summed in bfloat16 or wider, within the bound.
No kernel may reach another device: no remote copies, remote signals or barrier semaphores. Data moves between devices by JAX's collectives and lax.ppermute only.
A program may use at most 128 MiB of HBM per device.

v0:
```python
import jax
import jax.numpy as jnp
from jax import lax
from jax.sharding import PartitionSpec as P

stencil_taps = (1225.0 / 1024.0, -245.0 / 3072.0, 49.0 / 5120.0, -5.0 / 7168.0)
misfit_weight = 16.0
wave_rim = 8


def with_halo(block, sides, width):
    for axis, dim in sides:
        count = lax.axis_size(axis)
        forward = [(i, i + 1) for i in range(count - 1)]
        backward = [(target, source) for source, target in forward]
        low = lax.ppermute(
            lax.slice_in_dim(block, block.shape[dim] - width, None, axis=dim), axis, forward
        )
        high = lax.ppermute(lax.slice_in_dim(block, 0, width, axis=dim), axis, backward)
        block = jnp.concatenate([low, block, high], axis=dim)
    return block


def take_slab(array, first_index, length, which_axis):
    return lax.slice_in_dim(array, first_index, first_index + length, axis=which_axis)


def inner_part(array, which_axis):
    for other_axis in range(3):
        if other_axis != which_axis:
            array = take_slab(array, wave_rim, array.shape[other_axis] - 2 * wave_rim, other_axis)
    return array


def face_slope(array, which_axis):
    length = array.shape[which_axis] - 2 * wave_rim
    summed = jnp.zeros_like(take_slab(array, 0, length + 8, which_axis))
    for tap_index in range(1, 5):
        upper = take_slab(array, 3 + tap_index, length + 8, which_axis)
        lower = take_slab(array, 4 - tap_index, length + 8, which_axis)
        summed = summed + stencil_taps[tap_index - 1] * (upper - lower)
    return summed


def operate(wavefield_pad, buoyancy_pad):
    summed = 0.0
    for which_axis in range(3):
        field_part = inner_part(wavefield_pad, which_axis)
        weight_part = inner_part(buoyancy_pad, which_axis)
        length = field_part.shape[which_axis] - 2 * wave_rim
        face_weight = 0.5 * (
            take_slab(weight_part, 3, length + 8, which_axis)
            + take_slab(weight_part, 4, length + 8, which_axis)
        )
        face_flux = face_weight * face_slope(field_part, which_axis)
        for tap_index in range(1, 5):
            upper = take_slab(face_flux, 4 + tap_index, length, which_axis)
            lower = take_slab(face_flux, 5 - tap_index, length, which_axis)
            summed = summed + stencil_taps[tap_index - 1] * (upper - lower)
    return summed


def buoyancy_slope(scaled_pad, wavefield_pad):
    summed = 0.0
    for which_axis in range(3):
        scaled_part = inner_part(scaled_pad, which_axis)
        length = scaled_part.shape[which_axis] - 2 * wave_rim
        face_product = -face_slope(scaled_part, which_axis) * face_slope(
            inner_part(wavefield_pad, which_axis), which_axis
        )
        summed = summed + 0.5 * (
            take_slab(face_product, 4, length, which_axis)
            + take_slab(face_product, 5, length, which_axis)
        )
    return summed


def brick_rims(stacked):
    widened = with_halo(stacked, (("brick", 1),), 8)
    return jnp.pad(widened, ((0, 0), (0, 0), (wave_rim, wave_rim), (wave_rim, wave_rim)))


def tile_rims(array):
    widened = with_halo(array, (("shot", 2), ("brick", 1)), 1)
    return jnp.pad(widened, ((0, 0), (0, 0), (0, 0), (1, 1)))


def kernel_shifts():
    listed = []
    for shift_x in range(3):
        for shift_y in range(3):
            for shift_z in range(3):
                listed.append((9 * shift_x + 3 * shift_y + shift_z, shift_x, shift_y, shift_z))
    return listed


def conv_forward(padded, weights):
    extent = [padded.shape[dim_index] - 2 for dim_index in range(1, 4)]
    summed = 0.0
    for kernel_index, shift_x, shift_y, shift_z in kernel_shifts():
        window = padded[
            :,
            shift_x : shift_x + extent[0],
            shift_y : shift_y + extent[1],
            shift_z : shift_z + extent[2],
        ]
        summed = summed + jnp.einsum(
            "oc,cxyz->oxyz", weights[kernel_index], window, preferred_element_type=jnp.float32
        )
    return summed


def conv_back(grad_pad, weights):
    extent = [grad_pad.shape[dim_index] - 2 for dim_index in range(1, 4)]
    summed = 0.0
    for kernel_index, shift_x, shift_y, shift_z in kernel_shifts():
        window = grad_pad[
            :,
            2 - shift_x : 2 - shift_x + extent[0],
            2 - shift_y : 2 - shift_y + extent[1],
            2 - shift_z : 2 - shift_z + extent[2],
        ]
        summed = summed + jnp.einsum(
            "oc,oxyz->cxyz", weights[kernel_index], window, preferred_element_type=jnp.float32
        )
    return summed


def weight_grad(grads, padded):
    extent = grads.shape[1:]
    listed = []
    for kernel_index, shift_x, shift_y, shift_z in kernel_shifts():
        window = padded[
            :,
            shift_x : shift_x + extent[0],
            shift_y : shift_y + extent[1],
            shift_z : shift_z + extent[2],
        ]
        listed.append(
            jnp.einsum("oxyz,cxyz->oc", grads, window, preferred_element_type=jnp.float32)
        )
    return jnp.stack(listed)


def per_device(latent, conv_in, conv_out, source_field, observed, aperture, receivers):
    latent_pad = tile_rims(latent)
    hidden = jnp.tanh(conv_forward(latent_pad, conv_in)).astype(jnp.bfloat16)
    hidden_pad = tile_rims(hidden)
    output = conv_forward(hidden_pad, conv_out)
    squashed = jax.nn.sigmoid(output[0])
    modulus = 0.03 + 0.09 * squashed
    bent_part = jnp.tanh(output[1])
    buoyancy = jnp.exp(0.35 * bent_part)
    column = lax.all_gather(jnp.stack([modulus, buoyancy]), "shot", axis=2, tiled=True)
    first_row = aperture[0]
    window_rows = source_field.shape[2]
    window = lax.dynamic_slice_in_dim(column, first_row, window_rows, 2)
    brick_width = latent.shape[1]
    receiver_cells = receivers[0]
    local_x = receiver_cells[0] - lax.axis_index("brick") * brick_width
    owned_here = (local_x >= 0) & (local_x < brick_width)
    cell_x = jnp.clip(local_x, 0, brick_width - 1)
    cell_y = receiver_cells[1] - first_row
    cell_z = receiver_cells[2]
    recorded = observed[0]
    source = source_field[0]
    sections = recorded.shape[0]

    def inject(values):
        return jnp.zeros(source.shape, jnp.float32).at[cell_x, cell_y, cell_z].add(values)

    fields = []
    images = []
    residuals = []
    coefficient_pad = brick_rims(window)
    modulus_pad = coefficient_pad[0]
    buoyancy_pad = coefficient_pad[1]
    modulus_window = window[0]
    earlier = jnp.zeros_like(source)
    current = source
    for section_index in range(sections):
        wavefield_pad = brick_rims(current[None])[0]
        operated = operate(wavefield_pad, buoyancy_pad)
        following = 2.0 * current - earlier + modulus_window * operated
        fields.append(wavefield_pad)
        images.append(operated)
        misfit = misfit_weight * (following[cell_x, cell_y, cell_z] - recorded[len(residuals)])
        residuals.append(jnp.where(owned_here, misfit, 0.0))
        earlier = current
        current = following
    adjoint = inject(residuals[sections - 1])
    adjoint_later = jnp.zeros_like(source)
    grad_modulus = jnp.zeros_like(source)
    grad_buoyancy = jnp.zeros_like(source)
    for section_index in reversed(range(sections)):
        scaled_pad = modulus_pad * brick_rims(adjoint[None])[0]
        grad_modulus = grad_modulus + adjoint * images[section_index]
        grad_buoyancy = grad_buoyancy + buoyancy_slope(scaled_pad, fields[section_index])
        if section_index > 0:
            earlier_adjoint = (
                inject(residuals[section_index - 1])
                + 2.0 * adjoint
                + operate(scaled_pad, buoyancy_pad)
                - adjoint_later
            )
            adjoint_later = adjoint
            adjoint = earlier_adjoint
    column_grad = lax.dynamic_update_slice_in_dim(
        jnp.zeros(column.shape, jnp.float32), jnp.stack([grad_modulus, grad_buoyancy]), first_row, 2
    )
    tile_grad = lax.psum_scatter(column_grad, "shot", scatter_dimension=2, tiled=True)
    grad_output = jnp.stack(
        [
            tile_grad[0] * 0.09 * squashed * (1.0 - squashed),
            tile_grad[1] * buoyancy * 0.35 * (1.0 - bent_part * bent_part),
        ]
    ).astype(jnp.bfloat16)
    grad_hidden = conv_back(tile_rims(grad_output), conv_out)
    hidden_wide = hidden.astype(jnp.float32)
    grad_inner = (grad_hidden * (1.0 - hidden_wide * hidden_wide)).astype(jnp.bfloat16)
    grad_latent = conv_back(tile_rims(grad_inner), conv_in)
    grad_first = weight_grad(grad_inner, latent_pad)
    grad_second = weight_grad(grad_output, hidden_pad)
    grad_first, grad_second = lax.psum((grad_first, grad_second), ("shot", "brick"))
    return (grad_latent, grad_first, grad_second)


def solution(mesh):
    placed = (
        P(None, "brick", "shot", None),
        P(),
        P(),
        P("shot", "brick", None, None),
        P("shot", None, None),
        P("shot"),
        P("shot", None, None),
    )
    return jax.shard_map(
        per_device,
        mesh=mesh,
        in_specs=placed,
        out_specs=(P(None, "brick", "shot", None), P(), P()),
        check_vma=False,
    )
```

profile of v0, /device:TPU:32, one launch (start us, length us, event | category | flops | bytes accessed | tf_op | source)
XLA Modules:
  0.0 565.5 jit_solution(16717900112438961506)
XLA Ops:
  15.9 4.6 collective-permute-start.2
  20.5 3.6 collective-permute-start.3
  38.4 4.9 collective-permute-start.4
  46.8 3.7 collective-permute-start.6
  50.5 4.7 collective-permute-start.7
  79.7 5.9 %collective-permute-start.10 = (f32[1,8,16,128]{3,1,2,0:T(8,128)S(1)}, f32[1,8,16,128]{3,1,2,0:T(8,128)S(1)}, u32[]{:S(2)}, u32[]{:S(2)}) collective-permute-start(f32[1,8,16,128]{3,1,2,0:T(8,128)S(1)} %get-tuple-element.119), channel_id=1, source_target_pairs={{0,1},{1,2},{2,3},{3,4},{4,5},{5,6},{6,7},{8,9},{9,10},{10,11},{11... | collective-permute-start | bytes 196616 | tf_op jit(solution)/shard_map/ppermute | solution.py:16
  95.4 22.9 %all-gather.2.cloned.1.call-done = f32[2,32,32,128]{3,1,2,0:T(8,128)} async-done(((f32[2,32,2,128]{3,1,2,0:T(8,128)}), f32[2,32,32,128]{3,1,2,0:T(8,128)}) %all-gather.2.cloned.1.call-update) | async-done | bytes 1048592 | tf_op jit(solution)/shard_map/all_gather | solution.py:154
  119.3 4.7 collective-permute-start.8
  124.0 3.7 collective-permute-start.9
  142.0 4.6 collective-permute-start.12
  146.7 4.0 collective-permute-start.13
  150.7 3.6 collective-permute-done.13
  161.2 4.6 collective-permute-start.14
  165.8 3.7 collective-permute-start.15
  170.7 24.9 %gather_fusion.2 = f32[2048]{0:T(1024)} fusion(f32[32,16,128]{2,0,1:T(8,128)S(1)} %get-tuple-element.78, s32[2048]{0:T(1024)S(1)} %bitcast.1233), kind=kCustom, calls=%fused_computation.2 | custom fusion | bytes 40960 | tf_op jit(solution)/shard_map/gather | solution.py:187
  195.7 25.0 %gather_fusion.1 = f32[2048]{0:T(1024)} fusion(f32[32,16,128]{2,0,1:T(8,128)S(1)} %get-tuple-element.70, s32[2048]{0:T(1024)S(1)} %bitcast.1234), kind=kCustom, calls=%fused_computation.1 | custom fusion | bytes 40960 | tf_op jit(solution)/shard_map/gather | solution.py:187
  229.3 16.2 %gather_fusion = f32[2048]{0:T(1024)S(1)} fusion(f32[32,16,128]{2,0,1:T(8,128)S(1)} %get-tuple-element.62, s32[2048]{0:T(1024)S(1)} %bitcast.1235), kind=kCustom, calls=%fused_computation | custom fusion | bytes 40960 | tf_op jit(solution)/shard_map/gather | solution.py:187
  245.6 11.3 %scatter_custom_fusion = f32[65536]{0:T(1024)S(1)} fusion(s32[2048]{0:T(1024)S(1)} %broadcast_select_fusion, f32[2048]{0:T(1024)S(1)} %get-tuple-element.195, f32[]{:T(128)} %constant.19.clone.1), kind=kCustom, calls=%fused_computation.892 | custom fusion | flops 2048 | bytes 262148
  257.0 3.7 collective-permute-start.16
  260.7 4.9 collective-permute-start.17
  278.1 11.6 %scatter_fusion = f32[65536]{0:T(1024)S(1)} fusion(f32[65536]{0:T(1024)S(1)} %bitcast.1238, s32[2048]{0:T(1024)S(1)} %broadcast_select_fusion, f32[2048]{0:T(1024)S(1)} %get-tuple-element.194), kind=kCustom, calls=%fused_computation.4 | custom fusion | flops 2048 | bytes 32768
  289.9 5.2 collective-permute-start.18
  298.5 4.5 collective-permute-done.19
  312.5 11.6 %scatter_fusion.1 = f32[65536]{0:T(1024)S(1)} fusion(f32[65536]{0:T(1024)S(1)} %bitcast.1244, s32[2048]{0:T(1024)S(1)} %broadcast_select_fusion, f32[2048]{0:T(1024)S(1)} %get-tuple-element.193), kind=kCustom, calls=%fused_computation.5 | custom fusion | flops 2048 | bytes 32768
  325.6 3.7 collective-permute-start.20
  329.3 4.9 collective-permute-start.21
  344.9 61.2 %reduce-scatter.2.cloned.1.call-done = f32[2,32,2,128]{3,1,0,2:T(8,128)} async-done(((f32[2,32,32,128]{3,1,0,2:T(8,128)}), f32[2,32,2,128]{3,1,0,2:T(8,128)}) %reduce-scatter.2.cloned.1.call-update) | async-done | bytes 65552 | tf_op jit(solution)/shard_map/reduce_scatter | solution.py:211
  418.8 4.6 collective-permute-start.24
  423.4 3.9 collective-permute-start.25
  462.4 68.7 %all-reduce.11 = (f32[27,16,16]{2,1,0:T(8,128)S(1)}, f32[27,2,16]{2,1,0:T(2,128)S(1)}) all-reduce(f32[27,16,16]{2,1,0:T(8,128)S(1)} %fusion.84, f32[27,2,16]{2,1,0:T(2,128)S(1)} %fusion.111), channel_id=1, replica_groups=mesh['shot'=16,'brick'=8] {'shot','brick'}, use_global_device_ids=true, to_apply=%region_4.5 | all-reduce | flops 7776 | bytes 62208 | tf_op jit(solution)/shard_map/psum | solution.py:224
  532.6 4.5 collective-permute-start.29
  540.9 4.3 collective-permute-done.28
  (591 shorter events, 193.9 us)
Async XLA Ops:
  7.2 111.1 %all-gather.2.cloned.1.call-start = ((), (), s32[]{:S(2)}) async-start(), calls=%async_computation.1 | async-start | bytes 1114112 | tf_op jit(solution)/shard_map/all_gather | solution.py:154
  9.2 5.8 %collective-permute-start = (bf16[16,32,1,128]{3,0,2,1:T(8,128)(2,1)S(1)}, bf16[16,32,1,128]{3,0,2,1:T(8,128)(2,1)S(1)}, u32[]{:S(2)}, u32[]{:S(2)}) collective-permute-start(bf16[16,32,1,128]{3,0,2,1:T(8,128)(2,1)S(1)} %get-tuple-element.124), channel_id=1, source_target_pairs={{0,8},{8,16},{16,24},{24,32},{32,40},{40,48},{48,56},{56,64},{64,7... | collective-permute-start | bytes 393224 | tf_op jit(solution)/shard_map/ppermute | solution.py:16
  11.0 4.9 collective-permute-start.1
  15.9 15.5 %collective-permute-start.2 = (bf16[16,1,4,128]{3,0,2,1:T(8,128)(2,1)S(1)}, bf16[16,1,4,128]{3,0,2,1:T(8,128)(2,1)S(1)}, u32[]{:S(2)}, u32[]{:S(2)}) collective-permute-start(bf16[16,1,4,128]{3,0,2,1:T(8,128)(2,1)S(1)} %get-tuple-element.99), channel_id=1, source_target_pairs={{0,1},{1,2},{2,3},{3,4},{4,5},{5,6},{6,7},{8,9},{9,10},{10,11},{11... | collective-permute-start | bytes 49160 | tf_op jit(solution)/shard_map/ppermute | solution.py:16
  20.5 10.9 %collective-permute-start.3 = (bf16[16,1,4,128]{3,0,2,1:T(8,128)(2,1)S(1)}, bf16[16,1,4,128]{3,0,2,1:T(8,128)(2,1)S(1)}, u32[]{:S(2)}, u32[]{:S(2)}) collective-permute-start(bf16[16,1,4,128]{3,0,2,1:T(8,128)(2,1)S(1)} %get-tuple-element.100), channel_id=1, source_target_pairs={{1,0},{2,1},{3,2},{4,3},{5,4},{6,5},{7,6},{9,8},{10,9},{11,10},{12... | collective-permute-start | bytes 49160 | tf_op jit(solution)/shard_map/ppermute | solution.py:19
  38.4 6.4 %collective-permute-start.4 = (bf16[16,32,1,128]{3,0,2,1:T(8,128)(2,1)S(1)}, bf16[16,32,1,128]{3,0,2,1:T(8,128)(2,1)S(1)}, u32[]{:S(2)}, u32[]{:S(2)}) collective-permute-start(bf16[16,32,1,128]{3,0,2,1:T(8,128)(2,1)S(1)} %get-tuple-element.121), channel_id=1, source_target_pairs={{0,8},{8,16},{16,24},{24,32},{32,40},{40,48},{48,56},{56,64},{64,7... | collective-permute-start | bytes 393224 | tf_op jit(solution)/shard_map/ppermute | solution.py:16
  43.3 3.5 collective-permute-start.5
  46.8 8.8 %collective-permute-start.6 = (bf16[16,1,4,128]{3,0,2,1:T(8,128)(2,1)S(1)}, bf16[16,1,4,128]{3,0,2,1:T(8,128)(2,1)S(1)}, u32[]{:S(2)}, u32[]{:S(2)}) collective-permute-start(bf16[16,1,4,128]{3,0,2,1:T(8,128)(2,1)S(1)} %get-tuple-element.97), channel_id=1, source_target_pairs={{0,1},{1,2},{2,3},{3,4},{4,5},{5,6},{6,7},{8,9},{9,10},{10,11},{11... | collective-permute-start | bytes 49160 | tf_op jit(solution)/shard_map/ppermute | solution.py:16
  50.5 7.1 %collective-permute-start.7 = (bf16[16,1,4,128]{3,0,2,1:T(8,128)(2,1)S(1)}, bf16[16,1,4,128]{3,0,2,1:T(8,128)(2,1)S(1)}, u32[]{:S(2)}, u32[]{:S(2)}) collective-permute-start(bf16[16,1,4,128]{3,0,2,1:T(8,128)(2,1)S(1)} %get-tuple-element.98), channel_id=1, source_target_pairs={{1,0},{2,1},{3,2},{4,3},{5,4},{6,5},{7,6},{9,8},{10,9},{11,10},{12... | collective-permute-start | bytes 49160 | tf_op jit(solution)/shard_map/ppermute | solution.py:19
  79.5 326.6 %reduce-scatter.2.cloned.1.call-start = ((), (), s32[]{:S(2)}) async-start(), calls=%async_computation.2 | async-start | bytes 1114112 | tf_op jit(solution)/shard_map/reduce_scatter | solution.py:211
  79.7 12.4 %collective-permute-start.10 = (f32[1,8,16,128]{3,1,2,0:T(8,128)S(1)}, f32[1,8,16,128]{3,1,2,0:T(8,128)S(1)}, u32[]{:S(2)}, u32[]{:S(2)}) collective-permute-start(f32[1,8,16,128]{3,1,2,0:T(8,128)S(1)} %get-tuple-element.119), channel_id=1, source_target_pairs={{0,1},{1,2},{2,3},{3,4},{4,5},{5,6},{6,7},{8,9},{9,10},{10,11},{11... | collective-permute-start | bytes 196616 | tf_op jit(solution)/shard_map/ppermute | solution.py:16
  85.6 7.7 %collective-permute-start.11 = (f32[1,8,16,128]{3,1,2,0:T(8,128)S(1)}, f32[1,8,16,128]{3,1,2,0:T(8,128)S(1)}, u32[]{:S(2)}, u32[]{:S(2)}) collective-permute-start(f32[1,8,16,128]{3,1,2,0:T(8,128)S(1)} %get-tuple-element.120), channel_id=1, source_target_pairs={{1,0},{2,1},{3,2},{4,3},{5,4},{6,5},{7,6},{9,8},{10,9},{11,10},{12... | collective-permute-start | bytes 196616 | tf_op jit(solution)/shard_map/ppermute | solution.py:19
  119.3 10.1 %collective-permute-start.8 = (f32[2,8,16,128]{3,1,2,0:T(8,128)S(1)}, f32[2,8,16,128]{3,1,2,0:T(8,128)S(1)}, u32[]{:S(2)}, u32[]{:S(2)}) collective-permute-start(f32[2,8,16,128]{3,1,2,0:T(8,128)S(1)} %get-tuple-element.89), channel_id=1, source_target_pairs={{0,1},{1,2},{2,3},{3,4},{4,5},{5,6},{6,7},{8,9},{9,10},{10,11},{11... | collective-permute-start | bytes 393224 | tf_op jit(solution)/shard_map/ppermute | solution.py:16
  124.0 8.7 %collective-permute-start.9 = (f32[2,8,16,128]{3,1,2,0:T(8,128)S(1)}, f32[2,8,16,128]{3,1,2,0:T(8,128)S(1)}, u32[]{:S(2)}, u32[]{:S(2)}) collective-permute-start(f32[2,8,16,128]{3,1,2,0:T(8,128)S(1)} %get-tuple-element.90), channel_id=1, source_target_pairs={{1,0},{2,1},{3,2},{4,3},{5,4},{6,5},{7,6},{9,8},{10,9},{11,10},{12... | collective-permute-start | bytes 393224 | tf_op jit(solution)/shard_map/ppermute | solution.py:19
  142.0 8.7 %collective-permute-start.12 = (f32[1,8,16,128]{3,1,2,0:T(8,128)S(1)}, f32[1,8,16,128]{3,1,2,0:T(8,128)S(1)}, u32[]{:S(2)}, u32[]{:S(2)}) collective-permute-start(f32[1,8,16,128]{3,1,2,0:T(8,128)S(1)} %get-tuple-element.117), channel_id=1, source_target_pairs={{0,1},{1,2},{2,3},{3,4},{4,5},{5,6},{6,7},{8,9},{9,10},{10,11},{11... | collective-permute-start | bytes 196616 | tf_op jit(solution)/shard_map/ppermute | solution.py:16
  146.7 7.7 %collective-permute-start.13 = (f32[1,8,16,128]{3,1,2,0:T(8,128)S(1)}, f32[1,8,16,128]{3,1,2,0:T(8,128)S(1)}, u32[]{:S(2)}, u32[]{:S(2)}) collective-permute-start(f32[1,8,16,128]{3,1,2,0:T(8,128)S(1)} %get-tuple-element.118), channel_id=1, source_target_pairs={{1,0},{2,1},{3,2},{4,3},{5,4},{6,5},{7,6},{9,8},{10,9},{11,10},{12... | collective-permute-start | bytes 196616 | tf_op jit(solution)/shard_map/ppermute | solution.py:19
  161.2 59.5 %collective-permute-start.14 = (f32[1,8,16,128]{3,1,2,0:T(8,128)S(1)}, f32[1,8,16,128]{3,1,2,0:T(8,128)S(1)}, u32[]{:S(2)}, u32[]{:S(2)}) collective-permute-start(f32[1,8,16,128]{3,1,2,0:T(8,128)S(1)} %get-tuple-element.115), channel_id=1, source_target_pairs={{0,1},{1,2},{2,3},{3,4},{4,5},{5,6},{6,7},{8,9},{9,10},{10,11},{11... | collective-permute-start | bytes 196616 | tf_op jit(solution)/shard_map/ppermute | solution.py:16
  165.8 54.9 %collective-permute-start.15 = (f32[1,8,16,128]{3,1,2,0:T(8,128)S(1)}, f32[1,8,16,128]{3,1,2,0:T(8,128)S(1)}, u32[]{:S(2)}, u32[]{:S(2)}) collective-permute-start(f32[1,8,16,128]{3,1,2,0:T(8,128)S(1)} %get-tuple-element.116), channel_id=1, source_target_pairs={{1,0},{2,1},{3,2},{4,3},{5,4},{6,5},{7,6},{9,8},{10,9},{11,10},{12... | collective-permute-start | bytes 196616 | tf_op jit(solution)/shard_map/ppermute | solution.py:19
  257.0 8.6 %collective-permute-start.16 = (f32[1,8,16,128]{3,1,2,0:T(8,128)S(1)}, f32[1,8,16,128]{3,1,2,0:T(8,128)S(1)}, u32[]{:S(2)}, u32[]{:S(2)}) collective-permute-start(f32[1,8,16,128]{3,1,2,0:T(8,128)S(1)} %get-tuple-element.113), channel_id=1, source_target_pairs={{0,1},{1,2},{2,3},{3,4},{4,5},{5,6},{6,7},{8,9},{9,10},{10,11},{11... | collective-permute-start | bytes 196616 | tf_op jit(solution)/shard_map/ppermute | solution.py:16
  260.7 7.8 %collective-permute-start.17 = (f32[1,8,16,128]{3,1,2,0:T(8,128)S(1)}, f32[1,8,16,128]{3,1,2,0:T(8,128)S(1)}, u32[]{:S(2)}, u32[]{:S(2)}) collective-permute-start(f32[1,8,16,128]{3,1,2,0:T(8,128)S(1)} %get-tuple-element.114), channel_id=1, source_target_pairs={{1,0},{2,1},{3,2},{4,3},{5,4},{6,5},{7,6},{9,8},{10,9},{11,10},{12... | collective-permute-start | bytes 196616 | tf_op jit(solution)/shard_map/ppermute | solution.py:19
  289.9 8.6 %collective-permute-start.18 = (f32[1,8,16,128]{3,1,2,0:T(8,128)S(1)}, f32[1,8,16,128]{3,1,2,0:T(8,128)S(1)}, u32[]{:S(2)}, u32[]{:S(2)}) collective-permute-start(f32[1,8,16,128]{3,1,2,0:T(8,128)S(1)} %get-tuple-element.111), channel_id=1, source_target_pairs={{0,1},{1,2},{2,3},{3,4},{4,5},{5,6},{6,7},{8,9},{9,10},{10,11},{11... | collective-permute-start | bytes 196616 | tf_op jit(solution)/shard_map/ppermute | solution.py:16
  295.2 7.8 %collective-permute-start.19 = (f32[1,8,16,128]{3,1,2,0:T(8,128)S(1)}, f32[1,8,16,128]{3,1,2,0:T(8,128)S(1)}, u32[]{:S(2)}, u32[]{:S(2)}) collective-permute-start(f32[1,8,16,128]{3,1,2,0:T(8,128)S(1)} %get-tuple-element.112), channel_id=1, source_target_pairs={{1,0},{2,1},{3,2},{4,3},{5,4},{6,5},{7,6},{9,8},{10,9},{11,10},{12... | collective-permute-start | bytes 196616 | tf_op jit(solution)/shard_map/ppermute | solution.py:19
  325.6 8.6 %collective-permute-start.20 = (f32[1,8,16,128]{3,1,2,0:T(8,128)S(1)}, f32[1,8,16,128]{3,1,2,0:T(8,128)S(1)}, u32[]{:S(2)}, u32[]{:S(2)}) collective-permute-start(f32[1,8,16,128]{3,1,2,0:T(8,128)S(1)} %get-tuple-element.109), channel_id=1, source_target_pairs={{0,1},{1,2},{2,3},{3,4},{4,5},{5,6},{6,7},{8,9},{9,10},{10,11},{11... | collective-permute-start | bytes 196616 | tf_op jit(solution)/shard_map/ppermute | solution.py:16
  329.3 7.8 %collective-permute-start.21 = (f32[1,8,16,128]{3,1,2,0:T(8,128)S(1)}, f32[1,8,16,128]{3,1,2,0:T(8,128)S(1)}, u32[]{:S(2)}, u32[]{:S(2)}) collective-permute-start(f32[1,8,16,128]{3,1,2,0:T(8,128)S(1)} %get-tuple-element.110), channel_id=1, source_target_pairs={{1,0},{2,1},{3,2},{4,3},{5,4},{6,5},{7,6},{9,8},{10,9},{11,10},{12... | collective-permute-start | bytes 196616 | tf_op jit(solution)/shard_map/ppermute | solution.py:19
  407.0 2.6 collective-permute-start.22
  408.3 3.1 collective-permute-start.23
  418.8 8.8 %collective-permute-start.24 = (bf16[2,1,4,128]{3,1,2,0:T(2,128)(2,1)S(1)}, bf16[2,1,4,128]{3,1,2,0:T(2,128)(2,1)S(1)}, u32[]{:S(2)}, u32[]{:S(2)}) collective-permute-start(bf16[2,1,4,128]{3,1,2,0:T(2,128)(2,1)S(1)} %get-tuple-element.153), channel_id=1, source_target_pairs={{0,1},{1,2},{2,3},{3,4},{4,5},{5,6},{6,7},{8,9},{9,10},{10,11},{11... | collective-permute-start | bytes 6152 | tf_op jit(solution)/shard_map/ppermute | solution.py:16
  423.4 7.0 %collective-permute-start.25 = (bf16[2,1,4,128]{3,1,2,0:T(2,128)(2,1)S(1)}, bf16[2,1,4,128]{3,1,2,0:T(2,128)(2,1)S(1)}, u32[]{:S(2)}, u32[]{:S(2)}) collective-permute-start(bf16[2,1,4,128]{3,1,2,0:T(2,128)(2,1)S(1)} %get-tuple-element.154), channel_id=1, source_target_pairs={{1,0},{2,1},{3,2},{4,3},{5,4},{6,5},{7,6},{9,8},{10,9},{11,10},{12... | collective-permute-start | bytes 6152 | tf_op jit(solution)/shard_map/ppermute | solution.py:19
  459.2 73.4 %collective-permute-start.26 = (bf16[16,32,1,128]{3,0,2,1:T(8,128)(2,1)S(1)}, bf16[16,32,1,128]{3,0,2,1:T(8,128)(2,1)S(1)}, u32[]{:S(2)}, u32[]{:S(2)}) collective-permute-start(bf16[16,32,1,128]{3,0,2,1:T(8,128)(2,1)S(1)} %get-tuple-element.107), channel_id=1, source_target_pairs={{0,8},{8,16},{16,24},{24,32},{32,40},{40,48},{48,56},{56,64},{64,7... | collective-permute-start | bytes 393224 | tf_op jit(solution)/shard_map/ppermute | solution.py:16
  460.5 72.1 %collective-permute-start.27 = (bf16[16,32,1,128]{3,0,2,1:T(8,128)(2,1)S(1)}, bf16[16,32,1,128]{3,0,2,1:T(8,128)(2,1)S(1)}, u32[]{:S(2)}, u32[]{:S(2)}) collective-permute-start(bf16[16,32,1,128]{3,0,2,1:T(8,128)(2,1)S(1)} %get-tuple-element.108), channel_id=1, source_target_pairs={{8,0},{16,8},{24,16},{32,24},{40,32},{48,40},{56,48},{64,56},{72,6... | collective-permute-start | bytes 393224 | tf_op jit(solution)/shard_map/ppermute | solution.py:19
  532.6 8.2 %collective-permute-start.29 = (bf16[16,1,4,128]{3,0,2,1:T(8,128)(2,1)S(1)}, bf16[16,1,4,128]{3,0,2,1:T(8,128)(2,1)S(1)}, u32[]{:S(2)}, u32[]{:S(2)}) collective-permute-start(bf16[16,1,4,128]{3,0,2,1:T(8,128)(2,1)S(1)} %get-tuple-element.92), channel_id=1, source_target_pairs={{1,0},{2,1},{3,2},{4,3},{5,4},{6,5},{7,6},{9,8},{10,9},{11,10},{12... | collective-permute-start | bytes 49160 | tf_op jit(solution)/shard_map/ppermute | solution.py:19
  537.2 8.0 %collective-permute-start.28 = (bf16[16,1,4,128]{3,0,2,1:T(8,128)(2,1)S(1)}, bf16[16,1,4,128]{3,0,2,1:T(8,128)(2,1)S(1)}, u32[]{:S(2)}, u32[]{:S(2)}) collective-permute-start(bf16[16,1,4,128]{3,0,2,1:T(8,128)(2,1)S(1)} %get-tuple-element.91), channel_id=1, source_target_pairs={{0,1},{1,2},{2,3},{3,4},{4,5},{5,6},{6,7},{8,9},{9,10},{10,11},{11... | collective-permute-start | bytes 49160 | tf_op jit(solution)/shard_map/ppermute | solution.py:16
  (132 other events, 1131.1 us)
Sparse Core Ops, SparseCore 0:
  79.6 38.5 all-gather.1
  345.1 61.0 reduce-scatter.1
where the time goes:
time: 575 us; the launch traced here: 566 us
  waiting for transfers between devices  116 us (20%)
  starting transfers between devices  106 us (18%)
  local copies, waits for them, and re-layouts  98.6 us (17%)
  other arithmetic  88.4 us (15%)
  matrix products  69.4 us (12%)
  blocking collectives  68.7 us (12%)
  between operations  17.5 us (3%)
    psum x1, blocking collectives, per_device(): lax.psum((grad_first, grad_second), ('shot', 'brick'))  68.7 us
    gather x3, local copies, waits for them, and re-layouts, per_device(): following[cell_x, cell_y, cell_z] - recorded[len(residuals)]  66.2 us
    reduce_scatter x1, waiting for transfers between devices, per_device(): lax.psum_scatter(column_grad, 'shot', scatter_dimension=2, tiled=True)  61.2 us
    ppermute x15, starting transfers between devices, with_halo(): lax.ppermute(lax.slice_in_dim(block, block.shape[dim] - width, None, axis...  57.8 us
    ppermute x15, starting transfers between devices, with_halo(): lax.ppermute(lax.slice_in_dim(block, 0, width, axis=dim), axis, backward)  48.6 us
    unnamed x6, other arithmetic  35.9 us
    dot_general x54, matrix products, conv_back(): jnp.einsum('oc,oxyz->cxyz', weights[kernel_index], window, preferred_elem...  29.4 us
    ppermute x15, waiting for transfers between devices, with_halo(): lax.ppermute(lax.slice_in_dim(block, 0, width, axis=dim), axis, backward)  27.5 us
  transfers between devices with their start and end apart: 32, of which 16 were waited for; matrix products, arithmetic and copies ran while one was open for 13% of the time, Pallas kernels for 0%

commit v1 on v0

--- a/solution.py
+++ b/solution.py
@@ -6,6 +6,11 @@
 stencil_taps = (1225.0 / 1024.0, -245.0 / 3072.0, 49.0 / 5120.0, -5.0 / 7168.0)
 misfit_weight = 16.0
 wave_rim = 8
+
+
+def by_each_axis(value, inner_axis, outer_axis):
+    inner = lax.psum(value, inner_axis)
+    return lax.psum(inner, outer_axis)
 
 
 def with_halo(block, sides, width):
@@ -221,7 +226,7 @@
     grad_latent = conv_back(tile_rims(grad_inner), conv_in)
     grad_first = weight_grad(grad_inner, latent_pad)
     grad_second = weight_grad(grad_output, hidden_pad)
-    grad_first, grad_second = lax.psum((grad_first, grad_second), ("shot", "brick"))
+    grad_first, grad_second = by_each_axis((grad_first, grad_second), "shot", "brick")
     return (grad_latent, grad_first, grad_second)
 
 

time: 575 us -> 607 us (1.056)
  blocking collectives: 68.7 us -> 101 us
    psum x1 -> x2, blocking collectives: 68.7 us -> 101 us  [the longest x1 58.3 us: by_each_axis(): inner = lax.psum(value, inner_axis)]
  transfers between devices with their start and end apart: 32 -> 32, of which waited for: 16 -> 16; matrix products, arithmetic and copies ran while one was open for 13% -> 12% of each run, Pallas kernels for 0% -> 0%
where the time goes in v1:
time: 607 us; the launch traced here: 596 us
  waiting for transfers between devices  115 us (19%)
  starting transfers between devices  106 us (17%)
  blocking collectives  101 us (17%)
  local copies, waits for them, and re-layouts  98.6 us (16%)
  other arithmetic  88.4 us (15%)
  matrix products  69.3 us (11%)
  between operations  17.5 us (3%)
    gather x3, local copies, waits for them, and re-layouts, per_device(): following[cell_x, cell_y, cell_z] - recorded[len(residuals)]  66.1 us
    reduce_scatter x1, waiting for transfers between devices, per_device(): lax.psum_scatter(column_grad, 'shot', scatter_dimension=2, tiled=True)  61.2 us
    ppermute x15, starting transfers between devices, with_halo(): lax.ppermute(lax.slice_in_dim(block, block.shape[dim] - width, None, axis...  59.7 us
    psum x1, blocking collectives, by_each_axis(): inner = lax.psum(value, inner_axis)  58.3 us
    ppermute x15, starting transfers between devices, with_halo(): lax.ppermute(lax.slice_in_dim(block, 0, width, axis=dim), axis, backward)  46.8 us
    psum x1, blocking collectives, by_each_axis(): return lax.psum(inner, outer_axis)  42.5 us
    unnamed x6, other arithmetic  36 us
    dot_general x54, matrix products, conv_back(): jnp.einsum('oc,oxyz->cxyz', weights[kernel_index], window, preferred_elem...  29.3 us
  transfers between devices with their start and end apart: 32, of which 16 were waited for; matrix products, arithmetic and copies ran while one was open for 12% of the time, Pallas kernels for 0%

profile of v1, /device:TPU:32, one launch (start us, length us, event | category | flops | bytes accessed | tf_op | source)
XLA Modules:
  0.0 596.5 jit_solution(981671229977143499)
XLA Ops:
  15.8 4.6 collective-permute-start.2
  20.5 3.6 collective-permute-start.3
  38.4 4.9 collective-permute-start.4
  46.8 3.7 collective-permute-start.6
  50.5 4.7 collective-permute-start.7
  79.6 5.9 collective-permute-start.10
  95.4 22.9 %all-gather.2.cloned.1.call-done = f32[2,32,32,128]{3,1,2,0:T(8,128)} async-done(((f32[2,32,2,128]{3,1,2,0:T(8,128)}), f32[2,32,32,128]{3,1,2,0:T(8,128)}) %all-gather.2.cloned.1.call-update) | async-done | bytes 1048592 | tf_op jit(solution)/shard_map/all_gather | solution.py:159
  119.2 4.7 collective-permute-start.8
  124.0 3.7 collective-permute-start.9
  142.0 4.6 collective-permute-start.12
  146.6 4.0 collective-permute-start.13
  150.7 3.6 collective-permute-done.13
  161.1 4.6 collective-permute-start.14
  165.7 3.6 collective-permute-start.15
  170.7 24.9 %gather_fusion.2 = f32[2048]{0:T(1024)} fusion(f32[32,16,128]{2,0,1:T(8,128)S(1)} %get-tuple-element.80, s32[2048]{0:T(1024)S(1)} %bitcast.1233), kind=kCustom, calls=%fused_computation.2 | custom fusion | bytes 40960 | tf_op jit(solution)/shard_map/gather | solution.py:192
  195.6 25.0 %gather_fusion.1 = f32[2048]{0:T(1024)} fusion(f32[32,16,128]{2,0,1:T(8,128)S(1)} %get-tuple-element.72, s32[2048]{0:T(1024)S(1)} %bitcast.1234), kind=kCustom, calls=%fused_computation.1 | custom fusion | bytes 40960 | tf_op jit(solution)/shard_map/gather | solution.py:192
  229.2 16.2 %gather_fusion = f32[2048]{0:T(1024)S(1)} fusion(f32[32,16,128]{2,0,1:T(8,128)S(1)} %get-tuple-element.64, s32[2048]{0:T(1024)S(1)} %bitcast.1235), kind=kCustom, calls=%fused_computation | custom fusion | bytes 40960 | tf_op jit(solution)/shard_map/gather | solution.py:192
  245.5 11.3 %scatter_custom_fusion = f32[65536]{0:T(1024)S(1)} fusion(s32[2048]{0:T(1024)S(1)} %broadcast_select_fusion, f32[2048]{0:T(1024)S(1)} %get-tuple-element.197, f32[]{:T(128)} %constant.19.clone.1), kind=kCustom, calls=%fused_computation.892 | custom fusion | flops 2048 | bytes 262148
  256.9 3.7 collective-permute-start.16
  260.6 4.8 collective-permute-start.17
  278.0 11.6 %scatter_fusion = f32[65536]{0:T(1024)S(1)} fusion(f32[65536]{0:T(1024)S(1)} %bitcast.1238, s32[2048]{0:T(1024)S(1)} %broadcast_select_fusion, f32[2048]{0:T(1024)S(1)} %get-tuple-element.196), kind=kCustom, calls=%fused_computation.4 | custom fusion | flops 2048 | bytes 32768
  289.8 5.2 collective-permute-start.18
  298.3 4.5 collective-permute-done.19
  312.4 11.6 %scatter_fusion.1 = f32[65536]{0:T(1024)S(1)} fusion(f32[65536]{0:T(1024)S(1)} %bitcast.1244, s32[2048]{0:T(1024)S(1)} %broadcast_select_fusion, f32[2048]{0:T(1024)S(1)} %get-tuple-element.195), kind=kCustom, calls=%fused_computation.5 | custom fusion | flops 2048 | bytes 32768
  325.4 3.7 collective-permute-start.20
  329.1 4.9 collective-permute-start.21
  344.8 61.2 %reduce-scatter.2.cloned.1.call-done = f32[2,32,2,128]{3,1,0,2:T(8,128)} async-done(((f32[2,32,32,128]{3,1,0,2:T(8,128)}), f32[2,32,2,128]{3,1,0,2:T(8,128)}) %reduce-scatter.2.cloned.1.call-update) | async-done | bytes 65552 | tf_op jit(solution)/shard_map/reduce_scatter | solution.py:216
  418.7 4.6 collective-permute-start.24
  423.3 3.9 collective-permute-start.25
  462.2 58.3 %all-reduce.11 = (f32[27,16,16]{2,1,0:T(8,128)S(1)}, f32[27,2,16]{2,1,0:T(2,128)S(1)}) all-reduce(f32[27,16,16]{2,1,0:T(8,128)S(1)} %fusion.84, f32[27,2,16]{2,1,0:T(2,128)S(1)} %fusion.111), channel_id=1, replica_groups=mesh['shot'=16,'brick'=8] {'shot'}, use_global_device_ids=true, to_apply=%region_4.5 | all-reduce | flops 7776 | bytes 62208 | tf_op jit(solution)/shard_map/psum | solution.py:12
  520.5 42.5 %all-reduce.12 = (f32[27,16,16]{2,1,0:T(8,128)S(1)}, f32[27,2,16]{2,1,0:T(2,128)S(1)}) all-reduce(f32[27,16,16]{2,1,0:T(8,128)S(1)} %get-tuple-element.45, f32[27,2,16]{2,1,0:T(2,128)S(1)} %get-tuple-element.46), channel_id=1, replica_groups=mesh['shot'=16,'brick'=8] {'brick'}, use_global_device_ids=true, to_apply=%region_5.6 | all-reduce | flops 7776 | bytes 62208 | tf_op jit(solution)/shard_map/psum | solution.py:13
  567.2 5.0 collective-permute-start.28
  (592 shorter events, 196.7 us)
Async XLA Ops:
  7.2 111.1 %all-gather.2.cloned.1.call-start = ((), (), s32[]{:S(2)}) async-start(), calls=%async_computation.1 | async-start | bytes 1114112 | tf_op jit(solution)/shard_map/all_gather | solution.py:159
  9.2 5.8 collective-permute-start
  11.0 4.9 collective-permute-start.1
  15.8 15.5 %collective-permute-start.2 = (bf16[16,1,4,128]{3,0,2,1:T(8,128)(2,1)S(1)}, bf16[16,1,4,128]{3,0,2,1:T(8,128)(2,1)S(1)}, u32[]{:S(2)}, u32[]{:S(2)}) collective-permute-start(bf16[16,1,4,128]{3,0,2,1:T(8,128)(2,1)S(1)} %get-tuple-element.101), channel_id=1, source_target_pairs={{0,1},{1,2},{2,3},{3,4},{4,5},{5,6},{6,7},{8,9},{9,10},{10,11},{11... | collective-permute-start | bytes 49160 | tf_op jit(solution)/shard_map/ppermute | solution.py:21
  20.5 10.9 %collective-permute-start.3 = (bf16[16,1,4,128]{3,0,2,1:T(8,128)(2,1)S(1)}, bf16[16,1,4,128]{3,0,2,1:T(8,128)(2,1)S(1)}, u32[]{:S(2)}, u32[]{:S(2)}) collective-permute-start(bf16[16,1,4,128]{3,0,2,1:T(8,128)(2,1)S(1)} %get-tuple-element.102), channel_id=1, source_target_pairs={{1,0},{2,1},{3,2},{4,3},{5,4},{6,5},{7,6},{9,8},{10,9},{11,10},{12... | collective-permute-start | bytes 49160 | tf_op jit(solution)/shard_map/ppermute | solution.py:24
  38.4 6.4 %collective-permute-start.4 = (bf16[16,32,1,128]{3,0,2,1:T(8,128)(2,1)S(1)}, bf16[16,32,1,128]{3,0,2,1:T(8,128)(2,1)S(1)}, u32[]{:S(2)}, u32[]{:S(2)}) collective-permute-start(bf16[16,32,1,128]{3,0,2,1:T(8,128)(2,1)S(1)} %get-tuple-element.123), channel_id=1, source_target_pairs={{0,8},{8,16},{16,24},{24,32},{32,40},{40,48},{48,56},{56,64},{64,7... | collective-permute-start | bytes 393224 | tf_op jit(solution)/shard_map/ppermute | solution.py:21
  43.3 3.4 collective-permute-start.5
  46.8 8.8 %collective-permute-start.6 = (bf16[16,1,4,128]{3,0,2,1:T(8,128)(2,1)S(1)}, bf16[16,1,4,128]{3,0,2,1:T(8,128)(2,1)S(1)}, u32[]{:S(2)}, u32[]{:S(2)}) collective-permute-start(bf16[16,1,4,128]{3,0,2,1:T(8,128)(2,1)S(1)} %get-tuple-element.99), channel_id=1, source_target_pairs={{0,1},{1,2},{2,3},{3,4},{4,5},{5,6},{6,7},{8,9},{9,10},{10,11},{11... | collective-permute-start | bytes 49160 | tf_op jit(solution)/shard_map/ppermute | solution.py:21
  50.5 7.1 %collective-permute-start.7 = (bf16[16,1,4,128]{3,0,2,1:T(8,128)(2,1)S(1)}, bf16[16,1,4,128]{3,0,2,1:T(8,128)(2,1)S(1)}, u32[]{:S(2)}, u32[]{:S(2)}) collective-permute-start(bf16[16,1,4,128]{3,0,2,1:T(8,128)(2,1)S(1)} %get-tuple-element.100), channel_id=1, source_target_pairs={{1,0},{2,1},{3,2},{4,3},{5,4},{6,5},{7,6},{9,8},{10,9},{11,10},{12... | collective-permute-start | bytes 49160 | tf_op jit(solution)/shard_map/ppermute | solution.py:24
  79.5 326.5 %reduce-scatter.2.cloned.1.call-start = ((), (), s32[]{:S(2)}) async-start(), calls=%async_computation.2 | async-start | bytes 1114112 | tf_op jit(solution)/shard_map/reduce_scatter | solution.py:216
  79.6 12.5 %collective-permute-start.10 = (f32[1,8,16,128]{3,1,2,0:T(8,128)S(1)}, f32[1,8,16,128]{3,1,2,0:T(8,128)S(1)}, u32[]{:S(2)}, u32[]{:S(2)}) collective-permute-start(f32[1,8,16,128]{3,1,2,0:T(8,128)S(1)} %get-tuple-element.121), channel_id=1, source_target_pairs={{0,1},{1,2},{2,3},{3,4},{4,5},{5,6},{6,7},{8,9},{9,10},{10,11},{11... | collective-permute-start | bytes 196616 | tf_op jit(solution)/shard_map/ppermute | solution.py:21
  85.5 7.7 %collective-permute-start.11 = (f32[1,8,16,128]{3,1,2,0:T(8,128)S(1)}, f32[1,8,16,128]{3,1,2,0:T(8,128)S(1)}, u32[]{:S(2)}, u32[]{:S(2)}) collective-permute-start(f32[1,8,16,128]{3,1,2,0:T(8,128)S(1)} %get-tuple-element.122), channel_id=1, source_target_pairs={{1,0},{2,1},{3,2},{4,3},{5,4},{6,5},{7,6},{9,8},{10,9},{11,10},{12... | collective-permute-start | bytes 196616 | tf_op jit(solution)/shard_map/ppermute | solution.py:24
  119.2 10.1 %collective-permute-start.8 = (f32[2,8,16,128]{3,1,2,0:T(8,128)S(1)}, f32[2,8,16,128]{3,1,2,0:T(8,128)S(1)}, u32[]{:S(2)}, u32[]{:S(2)}) collective-permute-start(f32[2,8,16,128]{3,1,2,0:T(8,128)S(1)} %get-tuple-element.91), channel_id=1, source_target_pairs={{0,1},{1,2},{2,3},{3,4},{4,5},{5,6},{6,7},{8,9},{9,10},{10,11},{11... | collective-permute-start | bytes 393224 | tf_op jit(solution)/shard_map/ppermute | solution.py:21
  124.0 8.7 %collective-permute-start.9 = (f32[2,8,16,128]{3,1,2,0:T(8,128)S(1)}, f32[2,8,16,128]{3,1,2,0:T(8,128)S(1)}, u32[]{:S(2)}, u32[]{:S(2)}) collective-permute-start(f32[2,8,16,128]{3,1,2,0:T(8,128)S(1)} %get-tuple-element.92), channel_id=1, source_target_pairs={{1,0},{2,1},{3,2},{4,3},{5,4},{6,5},{7,6},{9,8},{10,9},{11,10},{12... | collective-permute-start | bytes 393224 | tf_op jit(solution)/shard_map/ppermute | solution.py:24
  142.0 8.7 %collective-permute-start.12 = (f32[1,8,16,128]{3,1,2,0:T(8,128)S(1)}, f32[1,8,16,128]{3,1,2,0:T(8,128)S(1)}, u32[]{:S(2)}, u32[]{:S(2)}) collective-permute-start(f32[1,8,16,128]{3,1,2,0:T(8,128)S(1)} %get-tuple-element.119), channel_id=1, source_target_pairs={{0,1},{1,2},{2,3},{3,4},{4,5},{5,6},{6,7},{8,9},{9,10},{10,11},{11... | collective-permute-start | bytes 196616 | tf_op jit(solution)/shard_map/ppermute | solution.py:21
  146.6 7.7 %collective-permute-start.13 = (f32[1,8,16,128]{3,1,2,0:T(8,128)S(1)}, f32[1,8,16,128]{3,1,2,0:T(8,128)S(1)}, u32[]{:S(2)}, u32[]{:S(2)}) collective-permute-start(f32[1,8,16,128]{3,1,2,0:T(8,128)S(1)} %get-tuple-element.120), channel_id=1, source_target_pairs={{1,0},{2,1},{3,2},{4,3},{5,4},{6,5},{7,6},{9,8},{10,9},{11,10},{12... | collective-permute-start | bytes 196616 | tf_op jit(solution)/shard_map/ppermute | solution.py:24
  161.1 59.5 %collective-permute-start.14 = (f32[1,8,16,128]{3,1,2,0:T(8,128)S(1)}, f32[1,8,16,128]{3,1,2,0:T(8,128)S(1)}, u32[]{:S(2)}, u32[]{:S(2)}) collective-permute-start(f32[1,8,16,128]{3,1,2,0:T(8,128)S(1)} %get-tuple-element.117), channel_id=1, source_target_pairs={{0,1},{1,2},{2,3},{3,4},{4,5},{5,6},{6,7},{8,9},{9,10},{10,11},{11... | collective-permute-start | bytes 196616 | tf_op jit(solution)/shard_map/ppermute | solution.py:21
  165.7 54.8 %collective-permute-start.15 = (f32[1,8,16,128]{3,1,2,0:T(8,128)S(1)}, f32[1,8,16,128]{3,1,2,0:T(8,128)S(1)}, u32[]{:S(2)}, u32[]{:S(2)}) collective-permute-start(f32[1,8,16,128]{3,1,2,0:T(8,128)S(1)} %get-tuple-element.118), channel_id=1, source_target_pairs={{1,0},{2,1},{3,2},{4,3},{5,4},{6,5},{7,6},{9,8},{10,9},{11,10},{12... | collective-permute-start | bytes 196616 | tf_op jit(solution)/shard_map/ppermute | solution.py:24
  256.9 8.6 %collective-permute-start.16 = (f32[1,8,16,128]{3,1,2,0:T(8,128)S(1)}, f32[1,8,16,128]{3,1,2,0:T(8,128)S(1)}, u32[]{:S(2)}, u32[]{:S(2)}) collective-permute-start(f32[1,8,16,128]{3,1,2,0:T(8,128)S(1)} %get-tuple-element.115), channel_id=1, source_target_pairs={{0,1},{1,2},{2,3},{3,4},{4,5},{5,6},{6,7},{8,9},{9,10},{10,11},{11... | collective-permute-start | bytes 196616 | tf_op jit(solution)/shard_map/ppermute | solution.py:21
  260.6 7.8 %collective-permute-start.17 = (f32[1,8,16,128]{3,1,2,0:T(8,128)S(1)}, f32[1,8,16,128]{3,1,2,0:T(8,128)S(1)}, u32[]{:S(2)}, u32[]{:S(2)}) collective-permute-start(f32[1,8,16,128]{3,1,2,0:T(8,128)S(1)} %get-tuple-element.116), channel_id=1, source_target_pairs={{1,0},{2,1},{3,2},{4,3},{5,4},{6,5},{7,6},{9,8},{10,9},{11,10},{12... | collective-permute-start | bytes 196616 | tf_op jit(solution)/shard_map/ppermute | solution.py:24
  289.8 8.6 %collective-permute-start.18 = (f32[1,8,16,128]{3,1,2,0:T(8,128)S(1)}, f32[1,8,16,128]{3,1,2,0:T(8,128)S(1)}, u32[]{:S(2)}, u32[]{:S(2)}) collective-permute-start(f32[1,8,16,128]{3,1,2,0:T(8,128)S(1)} %get-tuple-element.113), channel_id=1, source_target_pairs={{0,1},{1,2},{2,3},{3,4},{4,5},{5,6},{6,7},{8,9},{9,10},{10,11},{11... | collective-permute-start | bytes 196616 | tf_op jit(solution)/shard_map/ppermute | solution.py:21
  295.0 7.8 %collective-permute-start.19 = (f32[1,8,16,128]{3,1,2,0:T(8,128)S(1)}, f32[1,8,16,128]{3,1,2,0:T(8,128)S(1)}, u32[]{:S(2)}, u32[]{:S(2)}) collective-permute-start(f32[1,8,16,128]{3,1,2,0:T(8,128)S(1)} %get-tuple-element.114), channel_id=1, source_target_pairs={{1,0},{2,1},{3,2},{4,3},{5,4},{6,5},{7,6},{9,8},{10,9},{11,10},{12... | collective-permute-start | bytes 196616 | tf_op jit(solution)/shard_map/ppermute | solution.py:24
  325.4 8.6 %collective-permute-start.20 = (f32[1,8,16,128]{3,1,2,0:T(8,128)S(1)}, f32[1,8,16,128]{3,1,2,0:T(8,128)S(1)}, u32[]{:S(2)}, u32[]{:S(2)}) collective-permute-start(f32[1,8,16,128]{3,1,2,0:T(8,128)S(1)} %get-tuple-element.111), channel_id=1, source_target_pairs={{0,1},{1,2},{2,3},{3,4},{4,5},{5,6},{6,7},{8,9},{9,10},{10,11},{11... | collective-permute-start | bytes 196616 | tf_op jit(solution)/shard_map/ppermute | solution.py:21
  329.1 7.8 %collective-permute-start.21 = (f32[1,8,16,128]{3,1,2,0:T(8,128)S(1)}, f32[1,8,16,128]{3,1,2,0:T(8,128)S(1)}, u32[]{:S(2)}, u32[]{:S(2)}) collective-permute-start(f32[1,8,16,128]{3,1,2,0:T(8,128)S(1)} %get-tuple-element.112), channel_id=1, source_target_pairs={{1,0},{2,1},{3,2},{4,3},{5,4},{6,5},{7,6},{9,8},{10,9},{11,10},{12... | collective-permute-start | bytes 196616 | tf_op jit(solution)/shard_map/ppermute | solution.py:24
  406.8 2.6 collective-permute-start.22
  408.1 3.1 collective-permute-start.23
  418.7 8.8 %collective-permute-start.24 = (bf16[2,1,4,128]{3,1,2,0:T(2,128)(2,1)S(1)}, bf16[2,1,4,128]{3,1,2,0:T(2,128)(2,1)S(1)}, u32[]{:S(2)}, u32[]{:S(2)}) collective-permute-start(bf16[2,1,4,128]{3,1,2,0:T(2,128)(2,1)S(1)} %get-tuple-element.155), channel_id=1, source_target_pairs={{0,1},{1,2},{2,3},{3,4},{4,5},{5,6},{6,7},{8,9},{9,10},{10,11},{11... | collective-permute-start | bytes 6152 | tf_op jit(solution)/shard_map/ppermute | solution.py:21
  423.3 7.0 %collective-permute-start.25 = (bf16[2,1,4,128]{3,1,2,0:T(2,128)(2,1)S(1)}, bf16[2,1,4,128]{3,1,2,0:T(2,128)(2,1)S(1)}, u32[]{:S(2)}, u32[]{:S(2)}) collective-permute-start(bf16[2,1,4,128]{3,1,2,0:T(2,128)(2,1)S(1)} %get-tuple-element.156), channel_id=1, source_target_pairs={{1,0},{2,1},{3,2},{4,3},{5,4},{6,5},{7,6},{9,8},{10,9},{11,10},{12... | collective-permute-start | bytes 6152 | tf_op jit(solution)/shard_map/ppermute | solution.py:24
  459.1 105.5 %collective-permute-start.26 = (bf16[16,32,1,128]{3,0,2,1:T(8,128)(2,1)S(1)}, bf16[16,32,1,128]{3,0,2,1:T(8,128)(2,1)S(1)}, u32[]{:S(2)}, u32[]{:S(2)}) collective-permute-start(bf16[16,32,1,128]{3,0,2,1:T(8,128)(2,1)S(1)} %get-tuple-element.109), channel_id=1, source_target_pairs={{0,8},{8,16},{16,24},{24,32},{32,40},{40,48},{48,56},{56,64},{64,7... | collective-permute-start | bytes 393224 | tf_op jit(solution)/shard_map/ppermute | solution.py:21
  460.4 104.2 %collective-permute-start.27 = (bf16[16,32,1,128]{3,0,2,1:T(8,128)(2,1)S(1)}, bf16[16,32,1,128]{3,0,2,1:T(8,128)(2,1)S(1)}, u32[]{:S(2)}, u32[]{:S(2)}) collective-permute-start(bf16[16,32,1,128]{3,0,2,1:T(8,128)(2,1)S(1)} %get-tuple-element.110), channel_id=1, source_target_pairs={{8,0},{16,8},{24,16},{32,24},{40,32},{48,40},{56,48},{64,56},{72,6... | collective-permute-start | bytes 393224 | tf_op jit(solution)/shard_map/ppermute | solution.py:24
  564.6 8.2 %collective-permute-start.29 = (bf16[16,1,4,128]{3,0,2,1:T(8,128)(2,1)S(1)}, bf16[16,1,4,128]{3,0,2,1:T(8,128)(2,1)S(1)}, u32[]{:S(2)}, u32[]{:S(2)}) collective-permute-start(bf16[16,1,4,128]{3,0,2,1:T(8,128)(2,1)S(1)} %get-tuple-element.94), channel_id=1, source_target_pairs={{1,0},{2,1},{3,2},{4,3},{5,4},{6,5},{7,6},{9,8},{10,9},{11,10},{12... | collective-permute-start | bytes 49160 | tf_op jit(solution)/shard_map/ppermute | solution.py:24
  567.2 8.9 %collective-permute-start.28 = (bf16[16,1,4,128]{3,0,2,1:T(8,128)(2,1)S(1)}, bf16[16,1,4,128]{3,0,2,1:T(8,128)(2,1)S(1)}, u32[]{:S(2)}, u32[]{:S(2)}) collective-permute-start(bf16[16,1,4,128]{3,0,2,1:T(8,128)(2,1)S(1)} %get-tuple-element.93), channel_id=1, source_target_pairs={{0,1},{1,2},{2,3},{3,4},{4,5},{5,6},{6,7},{8,9},{9,10},{10,11},{11... | collective-permute-start | bytes 49160 | tf_op jit(solution)/shard_map/ppermute | solution.py:21
  (132 other events, 1132.7 us)
Sparse Core Ops, SparseCore 0:
  79.6 38.5 all-gather.1
  345.0 61.0 reduce-scatter.1
